TPU v7x, 32 devices: a whole 2x2x4 slice. The times are simulated.
32 devices in a mesh: dp: 8 (over y, x, core), tensor: 4 (over z).
Axes of the slice: x: 2, y: 2, z: 4, core: 2. Of those that a mesh axis runs over, the one named last changes fastest.
Arguments:
- inputs: bfloat16 [64, 256, 1152], P('dp'), may hold values from -6 to 6
- cotangent: bfloat16 [64, 256, 1152], P('dp'), may hold values from -6 to 6
- counts: int32 [8], P('dp'), may hold values from 1 to 8, as said below
- time_ids: int32 [64], P('dp'), may hold values from 0 to 999
- class_ids: int32 [64], P('dp'), may hold values from 0 to 1000
- time_table: bfloat16 [1000, 1152], replicated, may hold values from -4 to 4
- class_table: bfloat16 [1001, 1152], replicated, may hold values from -4 to 4
- ada_weight: bfloat16 [1152, 6, 1152], P(None, None, 'tensor'), may hold values from -0.1875 to 0.1875
- ada_bias: bfloat16 [6, 1152], P(None, 'tensor'), may hold values from -1.75 to 1.75
- qkv_weight: bfloat16 [1152, 3, 1152], P(None, None, 'tensor'), may hold values from -0.1875 to 0.1875
- qv_bias: bfloat16 [2, 1152], P(None, 'tensor'), may hold values from -1.75 to 1.75
- proj_weight: bfloat16 [1152, 1152], P('tensor'), may hold values from -1.5 to 1.5
- proj_bias: bfloat16 [1152], replicated, may hold values from -1.75 to 1.75
- up_weight: bfloat16 [1152, 4608], P(None, 'tensor'), may hold values from -0.1875 to 0.1875
- up_bias: bfloat16 [4608], P('tensor'), may hold values from -1.75 to 1.75
- down_weight: bfloat16 [4608, 1152], P('tensor'), may hold values from -0.09375 to 0.09375
- down_bias: bfloat16 [1152], replicated, may hold values from -1.75 to 1.75
Outputs:
- outputs: bfloat16 [64, 256, 1152], P('dp')
- grad_inputs: bfloat16 [64, 256, 1152], P('dp')
- grad_time_table: float32 [1000, 1152], replicated
- grad_class_table: float32 [1001, 1152], replicated
- grad_ada_weight: float32 [1152, 6, 1152], P(None, None, 'tensor')
- grad_ada_bias: float32 [6, 1152], P(None, 'tensor')
- grad_qkv_weight: float32 [1152, 3, 1152], P(None, None, 'tensor')
- grad_qv_bias: float32 [2, 1152], P(None, 'tensor')
- grad_proj_weight: float32 [1152, 1152], P('tensor')
- grad_proj_bias: float32 [1152], replicated
- grad_up_weight: float32 [1152, 4608], P(None, 'tensor')
- grad_up_bias: float32 [4608], P('tensor')
- grad_down_weight: float32 [4608, 1152], P('tensor')
- grad_down_bias: float32 [1152], replicated
Inputs may be any that keep to these rules, and one draw needn't show every extreme that they name: Each index of dp holds 8 image slots whose first counts live; at least one index has all 8 live.
All inputs are finite; a program needn't handle non-finite values.
Results may differ from a plain program's by a relative error of at most 0.014.
The roundings to bfloat16 on the way count: a program that leaves them out, or rounds other values in their place, can miss the bound.
Values sent between devices are 32-bit elements; how exact they have to be, the bound alone decides.
No kernel may reach another device: no remote copies, remote signals or barrier semaphores. Data moves between devices by JAX's collectives and lax.ppermute only.
A program may use at most 256 MiB of HBM per device.

v0:
```python
import jax
import jax.numpy as jnp
from jax import lax
from jax.sharding import PartitionSpec as P

HEAD_DIM = 72
EPSILON = 1e-06
GELU_ROOT = 0.7978845608028654
GELU_CUBIC = 0.044715


def norm_parts(values):
    average = jnp.mean(values, axis=-1, keepdims=True)
    centred = values - average
    spread = jnp.mean(centred * centred, axis=-1, keepdims=True)
    inverse = lax.rsqrt(spread + EPSILON)
    return (centred * inverse, inverse)


def norm_back(upstream, normed, inverse):
    first_mean = jnp.mean(upstream, axis=-1, keepdims=True)
    second_mean = jnp.mean(upstream * normed, axis=-1, keepdims=True)
    return inverse * (upstream - first_mean - normed * second_mean)


def gelu_parts(values):
    argument = GELU_ROOT * (values + GELU_CUBIC * values * values * values)
    tangent = jnp.tanh(argument)
    result = 0.5 * values * (1.0 + tangent)
    derivative = 0.5 * (1.0 + tangent) + 0.5 * values * (1.0 - tangent * tangent) * GELU_ROOT * (
        1.0 + 3.0 * GELU_CUBIC * values * values
    )
    return (result, derivative)


def local(
    inputs,
    cotangent,
    counts,
    time_ids,
    class_ids,
    time_table,
    class_table,
    ada_weight,
    ada_bias,
    qkv_weight,
    qv_bias,
    proj_weight,
    proj_bias,
    up_weight,
    up_bias,
    down_weight,
    down_bias,
):
    wide = jnp.float32
    narrow = jnp.bfloat16
    images, length, width = inputs.shape
    local_width = qkv_weight.shape[2]
    heads_here = local_width // HEAD_DIM
    scaling = HEAD_DIM ** (-0.5)
    live = (jnp.arange(images, dtype=jnp.int32) < counts[0]).astype(wide)
    time_levels = jnp.arange(time_table.shape[0], dtype=jnp.int32)
    class_levels = jnp.arange(class_table.shape[0], dtype=jnp.int32)
    time_pick = (time_ids[:, None] == time_levels[None, :]).astype(narrow)
    class_pick = (class_ids[:, None] == class_levels[None, :]).astype(narrow)
    condition = jnp.dot(time_pick, time_table, preferred_element_type=wide) + jnp.dot(
        class_pick, class_table, preferred_element_type=wide
    )
    silu_cond = jax.nn.silu(condition).astype(narrow)
    mod_local = jnp.einsum(
        "gd,dke->gke", silu_cond, ada_weight, preferred_element_type=wide
    ) + ada_bias.astype(wide)
    modulation = lax.all_gather(mod_local, "tensor", axis=2, tiled=True)
    shift_attn = modulation[:, 0, None, :]
    scale_attn = modulation[:, 1, None, :]
    gate_attn = modulation[:, 2, None, :]
    shift_mlp = modulation[:, 3, None, :]
    scale_mlp = modulation[:, 4, None, :]
    gate_mlp = modulation[:, 5, None, :]
    input_wide = inputs.astype(wide)
    normed_attn, inverse_attn = norm_parts(input_wide)
    hidden_attn = (normed_attn * (1.0 + scale_attn) + shift_attn).astype(narrow)
    projected = jnp.einsum("gsd,dke->gske", hidden_attn, qkv_weight, preferred_element_type=wide)
    bias_wide = qv_bias.astype(wide)
    shape_heads = (images, length, heads_here, HEAD_DIM)
    query_heads = (projected[:, :, 0] + bias_wide[0]).astype(narrow).reshape(shape_heads)
    key_heads = projected[:, :, 1].astype(narrow).reshape(shape_heads)
    value_heads = (projected[:, :, 2] + bias_wide[1]).astype(narrow).reshape(shape_heads)
    scores = (
        jnp.einsum("gqhe,gkhe->ghqk", query_heads, key_heads, preferred_element_type=wide) * scaling
    )
    highest = jnp.max(scores, axis=-1, keepdims=True)
    exponent = jnp.exp(scores - highest)
    denominator = jnp.sum(exponent, axis=-1, keepdims=True)
    soft_probs = (exponent / denominator).astype(narrow)
    log_total = highest + jnp.log(denominator)
    heads_out = jnp.einsum("ghqk,gkhe->gqhe", soft_probs, value_heads, preferred_element_type=wide)
    heads_out = heads_out.reshape(images, length, local_width).astype(narrow)
    attn_part = jnp.einsum("gse,ed->gsd", heads_out, proj_weight, preferred_element_type=wide)
    attention = lax.psum(attn_part, "tensor") + proj_bias.astype(wide)
    middle = input_wide + gate_attn * attention
    normed_mlp, inverse_mlp = norm_parts(middle)
    hidden_mlp = (normed_mlp * (1.0 + scale_mlp) + shift_mlp).astype(narrow)
    pre_act = jnp.einsum(
        "gsd,df->gsf", hidden_mlp, up_weight, preferred_element_type=wide
    ) + up_bias.astype(wide)
    gelu_value, gelu_slope = gelu_parts(pre_act)
    activated = gelu_value.astype(narrow)
    mlp_part = jnp.einsum("gsf,fd->gsd", activated, down_weight, preferred_element_type=wide)
    branch = lax.psum(mlp_part, "tensor") + down_bias.astype(wide)
    outputs = ((middle + gate_mlp * branch) * live[:, None, None]).astype(narrow)
    grad_out = cotangent.astype(wide) * live[:, None, None]
    d_gate_mlp = jnp.sum(grad_out * branch, axis=1)
    d_branch = (gate_mlp * grad_out).astype(narrow)
    grad_down_bias = jnp.sum(d_branch, axis=(0, 1), dtype=wide)
    grad_down_weight = jnp.einsum("gsf,gsd->fd", activated, d_branch, preferred_element_type=wide)
    d_activated = jnp.einsum("gsd,fd->gsf", d_branch, down_weight, preferred_element_type=wide)
    d_pre = (d_activated * gelu_slope).astype(narrow)
    grad_up_bias = jnp.sum(d_pre, axis=(0, 1), dtype=wide)
    grad_up_weight = jnp.einsum("gsd,gsf->df", hidden_mlp, d_pre, preferred_element_type=wide)
    grad_down_weight, grad_down_bias, grad_up_weight, grad_up_bias = lax.psum(
        (grad_down_weight, grad_down_bias, grad_up_weight, grad_up_bias), "dp"
    )
    d_mlp_part = jnp.einsum("gsf,df->gsd", d_pre, up_weight, preferred_element_type=wide)
    d_hidden_mlp = lax.psum(d_mlp_part, "tensor")
    d_shift_mlp = jnp.sum(d_hidden_mlp, axis=1)
    d_scale_mlp = jnp.sum(d_hidden_mlp * normed_mlp, axis=1)
    d_middle = grad_out + norm_back(d_hidden_mlp * (1.0 + scale_mlp), normed_mlp, inverse_mlp)
    d_gate_attn = jnp.sum(d_middle * attention, axis=1)
    d_attention = (gate_attn * d_middle).astype(narrow)
    grad_proj_bias = jnp.sum(d_attention, axis=(0, 1), dtype=wide)
    grad_proj_weight = jnp.einsum(
        "gse,gsd->ed", heads_out, d_attention, preferred_element_type=wide
    )
    d_heads = jnp.einsum("gsd,ed->gse", d_attention, proj_weight, preferred_element_type=wide)
    d_heads = d_heads.astype(narrow).reshape(shape_heads)
    scores_again = (
        jnp.einsum("gqhe,gkhe->ghqk", query_heads, key_heads, preferred_element_type=wide) * scaling
    )
    probs_again = jnp.exp(scores_again - log_total)
    d_value = jnp.einsum(
        "ghqk,gqhe->gkhe", probs_again.astype(narrow), d_heads, preferred_element_type=wide
    )
    d_value = d_value.astype(narrow)
    d_probs = jnp.einsum("gqhe,gkhe->ghqk", d_heads, value_heads, preferred_element_type=wide)
    row_inner = jnp.sum(probs_again * d_probs, axis=-1, keepdims=True)
    d_scores = (probs_again * (d_probs - row_inner)).astype(narrow)
    d_query = (
        jnp.einsum("ghqk,gkhe->gqhe", d_scores, key_heads, preferred_element_type=wide) * scaling
    ).astype(narrow)
    d_key = (
        jnp.einsum("ghqk,gqhe->gkhe", d_scores, query_heads, preferred_element_type=wide) * scaling
    ).astype(narrow)
    d_projected = jnp.stack([d_query, d_key, d_value], axis=2).reshape(
        images, length, 3, local_width
    )
    grad_qv_bias = jnp.stack(
        [
            jnp.sum(d_query, axis=(0, 1), dtype=wide).reshape(local_width),
            jnp.sum(d_value, axis=(0, 1), dtype=wide).reshape(local_width),
        ],
        axis=0,
    )
    grad_qkv_weight = jnp.einsum(
        "gsd,gske->dke", hidden_attn, d_projected, preferred_element_type=wide
    )
    d_attn_part = jnp.einsum("gske,dke->gsd", d_projected, qkv_weight, preferred_element_type=wide)
    d_hidden_attn = lax.psum(d_attn_part, "tensor")
    d_shift_attn = jnp.sum(d_hidden_attn, axis=1)
    d_scale_attn = jnp.sum(d_hidden_attn * normed_attn, axis=1)
    grad_inputs = (
        d_middle + norm_back(d_hidden_attn * (1.0 + scale_attn), normed_attn, inverse_attn)
    ).astype(narrow)
    d_modulation = jnp.stack(
        [d_shift_attn, d_scale_attn, d_gate_attn, d_shift_mlp, d_scale_mlp, d_gate_mlp], axis=1
    ).astype(narrow)
    start_column = lax.axis_index("tensor") * local_width
    d_mod_local = lax.dynamic_slice_in_dim(d_modulation, start_column, local_width, 2)
    grad_ada_weight = jnp.einsum("gd,gke->dke", silu_cond, d_mod_local, preferred_element_type=wide)
    grad_ada_bias = jnp.sum(d_mod_local, axis=0, dtype=wide)
    (
        grad_qkv_weight,
        grad_qv_bias,
        grad_proj_weight,
        grad_proj_bias,
        grad_ada_weight,
        grad_ada_bias,
    ) = lax.psum(
        (
            grad_qkv_weight,
            grad_qv_bias,
            grad_proj_weight,
            grad_proj_bias,
            grad_ada_weight,
            grad_ada_bias,
        ),
        "dp",
    )
    sigmoid_cond = jax.nn.sigmoid(condition)
    d_condition = jnp.einsum("gke,dke->gd", d_mod_local, ada_weight, preferred_element_type=wide)
    d_condition = d_condition * sigmoid_cond * (1.0 + condition * (1.0 - sigmoid_cond))
    exact = lax.Precision.HIGHEST
    grad_time_table = jnp.dot(time_pick.astype(wide).T, d_condition, precision=exact)
    grad_class_table = jnp.dot(class_pick.astype(wide).T, d_condition, precision=exact)
    grad_time_table, grad_class_table = lax.psum(
        (grad_time_table, grad_class_table), ("dp", "tensor")
    )
    return (
        outputs,
        grad_inputs,
        grad_time_table,
        grad_class_table,
        grad_ada_weight,
        grad_ada_bias,
        grad_qkv_weight,
        grad_qv_bias,
        grad_proj_weight,
        grad_proj_bias,
        grad_up_weight,
        grad_up_bias,
        grad_down_weight,
        grad_down_bias,
    )


def solution(mesh):
    in_specs = (
        P("dp", None, None),
        P("dp", None, None),
        P("dp"),
        P("dp"),
        P("dp"),
        P(),
        P(),
        P(None, None, "tensor"),
        P(None, "tensor"),
        P(None, None, "tensor"),
        P(None, "tensor"),
        P("tensor", None),
        P(),
        P(None, "tensor"),
        P("tensor"),
        P("tensor", None),
        P(),
    )
    out_specs = (
        P("dp", None, None),
        P("dp", None, None),
        P(),
        P(),
        P(None, None, "tensor"),
        P(None, "tensor"),
        P(None, None, "tensor"),
        P(None, "tensor"),
        P("tensor", None),
        P(),
        P(None, "tensor"),
        P("tensor"),
        P("tensor", None),
        P(),
    )
    return jax.shard_map(local, mesh=mesh, in_specs=in_specs, out_specs=out_specs, check_vma=False)
```

profile of v0, /device:TPU:0, one launch (start us, length us, event | category | flops | bytes accessed | tf_op | source)
XLA Modules:
  0.0 2098.7 jit_solution(2705256795855632784)
XLA Ops:
  10.5 4.5 fusion.14
  19.4 91.1 %all_gather.3 = f32[8,6,1152]{1,0,2:T(8,128)} all-gather(f32[8,6,288]{1,0,2:T(8,128)} %copy.58), channel_id=1, replica_groups=mesh['dp'=8,'tensor'=4] {'tensor'}, dimensions={2}, use_global_device_ids=true | all-gather | bytes 276480 | tf_op jit(solution)/shard_map/all_gather | solution.py:73
  110.5 22.1 %fusion.73 = (f32[8,1,1152]{1,0,2:T(8,128)}, f32[8,1,1152]{1,0,2:T(8,128)}, f32[8,1,1152]{1,0,2:T(8,128)}, f32[8,1,1152]{1,0,2:T(8,128)}, f32[8,1,1152]{1,0,2:T(8,128)}, /*index=5*/f32[8,1,1152]{1,0,2:T(8,128)}) fusion(f32[8,6,1152]{1,0,2:T(8,128)} %all_gather.3), kind=kLoop, calls=%fused_computation.140 | loop fusion | bytes 442368 | tf_op jit(solution)/shard_map/slice | solution.py:79
  139.3 7.8 fusion.40
  159.6 5.4 fusion.49
  180.0 310.3 %all-reduce.10.cloned.1.call-done = f32[8,256,1152]{2,1,0:T(8,128)} async-done(((f32[8,256,1152]{2,1,0:T(8,128)}), f32[8,256,1152]{2,1,0:T(8,128)}) %all-reduce.10.cloned.1.call-update) | async-done | bytes 9437200 | tf_op jit(solution)/shard_map/psum | solution.py:100
  490.3 10.4 fusion.71
  500.7 4.9 multiply_reduce_fusion.4
  507.1 9.6 fusion.35
  516.7 12.8 convert_reduce_fusion.2
  531.8 9.6 fusion.33
  542.2 13.1 fusion.31
  555.3 309.9 %all-reduce.12.cloned.1.call-done = f32[8,256,1152]{2,1,0:T(8,128)} async-done(((f32[8,256,1152]{2,1,0:T(8,128)}), f32[8,256,1152]{2,1,0:T(8,128)}) %all-reduce.12.cloned.1.call-update) | async-done | bytes 9437200 | tf_op jit(solution)/shard_map/psum | solution.py:125
  865.2 8.5 multiply_reduce_fusion.1
  874.4 11.4 convert_reduce_fusion.3
  900.4 7.9 convolution_bitcast_fusion.2
  909.1 16.6 convolution_bitcast_fusion
  925.7 611.2 %all-reduce.18.cloned.1.call-done = (f32[8,256,1152]{2,1,0:T(8,128)}, f32[8,256,1152]{2,1,0:T(8,128)}) async-done(((f32[8,256,1152]{2,1,0:T(8,128)}, f32[8,256,1152]{2,1,0:T(8,128)}), (f32[8,256,1152]{2,1,0:T(8,128)}, f32[8,256,1152]{2,1,0:T(8,128)})) %all-reduce.18.cloned.1.call-update) | async-done | bytes 18874384 | tf_op jit(solution)/shard_map/psum | solution.py:110
  1537.0 8.8 fusion.13
  1545.9 13.2 convert_reduce_fusion.1
  1559.3 9.1 multiply_reduce_fusion.2
  1569.2 4.4 fusion.54
  1573.6 4.3 fusion.53
  1578.4 15.1 convolution_bitcast_fusion.1
  1593.5 5.3 convolution_bitcast_fusion.4
  1598.8 9.8 convolution_bitcast_fusion.3
  1608.6 4.7 fusion.56
  1614.0 24.1 %all-reduce.1 = (f32[6,288]{1,0:T(8,128)}, f32[2,288]{1,0:T(2,128)}, f32[1152]{0:T(1024)}, f32[1152]{0:T(1024)}, f32[1152]{0:T(1024)}) all-reduce(f32[6,288]{1,0:T(8,128)S(1)} %convert_reduce_fusion.6, f32[2,288]{1,0:T(2,128)S(1)} %pad_maximum_fusion.3, f32[1152]{0:T(1024)S(1)} %copy-done.42, ...), channel_id=1, replica_groups=mesh['dp'=8,'tensor'=4] {'dp'}, use_global_device_ids=true, to_apply=%region_25.26 | all-reduce | flops 5760 | bytes 46080 | tf_op jit(solution)/shard_map/psum | solution.py:188
  1638.2 128.6 %all-reduce.14.cloned.1.call-done = (f32[1000,1152]{1,0:T(8,128)}, f32[1001,1152]{1,0:T(8,128)}) async-done(((f32[1000,1152]{1,0:T(8,128)}, f32[1001,1152]{1,0:T(8,128)}), (f32[1000,1152]{1,0:T(8,128)}, f32[1001,1152]{1,0:T(8,128)})) %all-reduce.14.cloned.1.call-update) | async-done | bytes 9220624 | tf_op jit(solution)/shard_map/psum | solution.py:205
  1766.7 300.5 %all-reduce.16.cloned.1.call-done = (f32[1152,6,288]{0,2,1:T(8,128)}, f32[1152,3,288]{0,2,1:T(8,128)}, f32[288,1152]{1,0:T(8,128)}, f32[1152,1152]{1,0:T(8,128)}, f32[1152,1152]{1,0:T(8,128)}) async-done(((f32[1152,6,288]{0,2,1:T(8,128)}, f32[1152,3,288]{0,2,1:T(8,128)}, f32[288,1152]{1,0:T(8,128)}, f32[1152,1152]{1,0:T(8,128)}, f32[1152,1152]{1,0:T(8,128)}), (f32[1152,6,288]{0,2,1:T(8,128)}, ...) | async-done | bytes 23887888 | tf_op jit(solution)/shard_map/psum | solution.py:188
  2067.2 5.1 copy.107
  2076.8 4.0 copy.109
  (231 shorter events, 78.9 us)
Async XLA Ops:
  7.2 509.5 %copy-start = (bf16[1152,1152]{1,0:T(8,128)(2,1)S(1)}, bf16[1152,1152]{1,0:T(8,128)(2,1)}, u32[]{:S(2)}) copy-start(bf16[1152,1152]{1,0:T(8,128)(2,1)} %param.32) | copy-start | bytes 7962628
  7.2 483.1 %all-reduce.10.cloned.1.call-start = ((), (), s32[]{:S(2)}) async-start(), calls=%async_computation | async-start | bytes 18874368 | tf_op jit(solution)/shard_map/psum | solution.py:100
  7.3 9.4 copy-start.6
  10.5 128.8 %copy-start.32 = (f32[8,256]{1,0:T(8,128)}, f32[8,256]{1,0:T(8,128)S(1)}, u32[]{:S(2)}) copy-start(f32[8,256]{1,0:T(8,128)S(1)} %broadcast_multiply_fusion.5) | copy-start | bytes 24580
  15.0 124.3 %copy-start.34 = (f32[8,256]{1,0:T(8,128)}, f32[8,256]{1,0:T(8,128)S(1)}, u32[]{:S(2)}) copy-start(f32[8,256]{1,0:T(8,128)S(1)} %add_rsqrt_fusion.1) | copy-start | bytes 24580
  135.9 11.2 copy-start.38
  165.0 700.2 %all-reduce.12.cloned.1.call-start = ((), (), s32[]{:S(2)}) async-start(), calls=%async_computation.1 | async-start | bytes 18874368 | tf_op jit(solution)/shard_map/psum | solution.py:125
  165.7 324.6 %copy-start.36 = (f32[1152]{0:T(1024)}, f32[1152]{0:T(1024)S(1)}, u32[]{:S(2)}) copy-start(f32[1152]{0:T(1024)S(1)} %convert_element_type.142) | copy-start | bytes 13828
  180.0 336.7 %copy-start.54 = (f32[8]{0:T(128)}, f32[8]{0:T(128)S(1)}, u32[]{:S(2)}) copy-start(f32[8]{0:T(128)S(1)} %compare_convert_fusion) | copy-start | bytes 100
  490.3 15.3 copy-start.57
  500.7 15.9 slice-start.10
  507.1 9.6 slice-start.11
  541.5 995.5 %all-reduce.18.cloned.1.call-start = ((), (), s32[]{:S(2)}) async-start(), calls=%async_computation.4 | async-start | bytes 37748736 | tf_op jit(solution)/shard_map/psum | solution.py:110
  555.3 318.4 %copy-start.55 = (f32[8]{0:T(128)S(1)}, f32[8]{0:T(128)}, u32[]{:S(2)}) copy-start(f32[8]{0:T(128)} %copy-done.54) | copy-start | bytes 100
  908.4 858.3 %all-reduce.14.cloned.1.call-start = ((), (), s32[]{:S(2)}) async-start(), calls=%async_computation.2 | async-start | bytes 18505728 | tf_op jit(solution)/shard_map/psum | solution.py:205
  909.1 627.9 %copy-start.29 = (f32[8,1152]{1,0:T(8,128)S(1)}, f32[8,1152]{1,0:T(8,128)}, u32[]{:S(2)}) copy-start(f32[8,1152]{1,0:T(8,128)} %copy-done.28) | copy-start | bytes 110596
  909.1 627.9 %copy-start.33 = (f32[8,256]{1,0:T(8,128)S(1)}, f32[8,256]{1,0:T(8,128)}, u32[]{:S(2)}) copy-start(f32[8,256]{1,0:T(8,128)} %copy-done.32) | copy-start | bytes 24580
  909.1 627.9 %copy-start.35 = (f32[8,256]{1,0:T(8,128)S(1)}, f32[8,256]{1,0:T(8,128)}, u32[]{:S(2)}) copy-start(f32[8,256]{1,0:T(8,128)} %copy-done.34) | copy-start | bytes 24580
  1537.0 22.2 %slice-start.2 = ((s8[4718592]{0:T(1024)(128)(4,1)}), s8[4194304]{0:T(1024)(128)(4,1)S(1)}, s32[]{:S(2)}) async-start(s8[4718592]{0:T(1024)(128)(4,1)} %bitcast.124), calls=%async_computation.7 | async-start | bytes 8388608
  1537.0 22.2 %slice-start.4 = ((s8[9437184]{0:T(1024)(128)(4,1)}), s8[4194304]{0:T(1024)(128)(4,1)S(1)}, s32[]{:S(2)}) async-start(s8[9437184]{0:T(1024)(128)(4,1)} %bitcast.126), calls=%async_computation.9 | async-start | bytes 8388608
  1537.0 22.2 %slice-start.5 = ((s8[9437184]{0:T(1024)(128)(4,1)}), s8[4194304]{0:T(1024)(128)(4,1)S(1)}, s32[]{:S(2)}) async-start(s8[9437184]{0:T(1024)(128)(4,1)} %bitcast.126), calls=%async_computation.10 | async-start | bytes 8388608
  1537.0 22.2 %slice-start.7 = ((s8[9437184]{0:T(1024)(128)(4,1)}), s8[4194304]{0:T(1024)(128)(4,1)S(1)}, s32[]{:S(2)}) async-start(s8[9437184]{0:T(1024)(128)(4,1)} %bitcast.128), calls=%async_computation.12 | async-start | bytes 8388608
  1537.0 22.2 %slice-start.8 = ((s8[9437184]{0:T(1024)(128)(4,1)}), s8[4194304]{0:T(1024)(128)(4,1)S(1)}, s32[]{:S(2)}) async-start(s8[9437184]{0:T(1024)(128)(4,1)} %bitcast.128), calls=%async_computation.13 | async-start | bytes 8388608
  1545.9 13.3 slice-start.3
  1545.9 13.3 slice-start.6
  1545.9 13.3 slice-start.9
  1545.9 13.3 copy-start.37
  1559.3 9.9 copy-start.51
  1569.2 9.2 copy-start.41
  1577.9 15.6 copy-start.18
  1577.9 489.3 %all-reduce.16.cloned.1.call-start = ((), (), s32[]{:S(2)}) async-start(), calls=%async_computation.3 | async-start | bytes 47775744 | tf_op jit(solution)/shard_map/psum | solution.py:188
  2072.3 12.5 slice-start.16
  (51 other events, 257.0 us)
Sparse Core Ops, SparseCore 0:
  165.1 325.1 all-reduce.9
  541.6 323.5 all-reduce.11
  908.5 628.3 all-reduce.17
  1578.0 188.6 all-reduce.13
  1772.5 294.6 all-reduce.15
where the time goes:
time: 2100 us
  waiting for transfers between devices  1660 us (79%)
  matrix products  144 us (7%)
  blocking collectives  115 us (5%)
  local copies, waits for them, and re-layouts  84.7 us (4%)
  other arithmetic  78.3 us (4%)
    psum x1, waiting for transfers between devices, local(): branch = lax.psum(mlp_part, 'tensor') + down_bias.astype(wide)  611 us
    psum x1, waiting for transfers between devices, local(): attention = lax.psum(attn_part, 'tensor') + proj_bias.astype(wide)  310 us
    psum x1, waiting for transfers between devices, local(): d_hidden_mlp = lax.psum(d_mlp_part, 'tensor')  310 us
    psum x1, waiting for transfers between devices, local(): lax.psum((grad_qkv_weight, grad_qv_bias, grad_proj_weight, grad_proj_bias...  300 us
    psum x1, waiting for transfers between devices, local(): lax.psum((grad_time_table, grad_class_table), ('dp', 'tensor'))  129 us
    all_gather x1, blocking collectives, local(): modulation = lax.all_gather(mod_local, 'tensor', axis=2, tiled=True)  91.1 us
    unnamed x174, local copies, waits for them, and re-layouts  57 us
  transfers between devices with their start and end apart: 5, of which 5 were waited for; matrix products, arithmetic and copies ran while one was open for 4% of the time, Pallas kernels for 0%

commit v1 on v0

--- a/solution.py
+++ b/solution.py
@@ -52,6 +52,10 @@
     down_weight,
     down_bias,
 ):
+
+    def waves_open(vector, named_axis):
+        return lax.all_gather(vector, named_axis).sum(axis=0)
+
     wide = jnp.float32
     narrow = jnp.bfloat16
     images, length, width = inputs.shape
@@ -122,7 +126,7 @@
         (grad_down_weight, grad_down_bias, grad_up_weight, grad_up_bias), "dp"
     )
     d_mlp_part = jnp.einsum("gsf,df->gsd", d_pre, up_weight, preferred_element_type=wide)
-    d_hidden_mlp = lax.psum(d_mlp_part, "tensor")
+    d_hidden_mlp = waves_open(d_mlp_part, "tensor")
     d_shift_mlp = jnp.sum(d_hidden_mlp, axis=1)
     d_scale_mlp = jnp.sum(d_hidden_mlp * normed_mlp, axis=1)
     d_middle = grad_out + norm_back(d_hidden_mlp * (1.0 + scale_mlp), normed_mlp, inverse_mlp)

time: 2100 us -> 2430 us (1.16)
  waiting for transfers between devices: 1660 us -> 1950 us
  other arithmetic: 78.3 us -> 109 us
    all_gather x0 -> x1, waiting for transfers between devices: none -> 616 us  [waves_open(): return lax.all_gather(vector, named_axis).sum(axis=0)]
    psum x1 -> x0, waiting for transfers between devices: 310 us -> none  [local(): d_hidden_mlp = lax.psum(d_mlp_part, 'tensor')]
    reduce_sum x0 -> x3, other arithmetic: none -> 31 us  [the longest x1 17.6 us: waves_open(): return lax.all_gather(vector, named_axis).sum(axis=0)]
    unnamed x174 -> x176, local copies, waits for them, and re-layouts: 57 us -> 57.3 us
where the time goes in v1:
time: 2430 us; the launch traced here: 2420 us
  waiting for transfers between devices  1950 us (80%)
  matrix products  145 us (6%)
  blocking collectives  115 us (5%)
  other arithmetic  109 us (4%)
  local copies, waits for them, and re-layouts  85 us (3%)
    all_gather x1, waiting for transfers between devices, waves_open(): return lax.all_gather(vector, named_axis).sum(axis=0)  616 us
    psum x1, waiting for transfers between devices, local(): branch = lax.psum(mlp_part, 'tensor') + down_bias.astype(wide)  597 us
    psum x1, waiting for transfers between devices, local(): attention = lax.psum(attn_part, 'tensor') + proj_bias.astype(wide)  310 us
    psum x1, waiting for transfers between devices, local(): lax.psum((grad_qkv_weight, grad_qv_bias, grad_proj_weight, grad_proj_bias...  300 us
    psum x1, waiting for transfers between devices, local(): lax.psum((grad_time_table, grad_class_table), ('dp', 'tensor'))  128 us
    all_gather x1, blocking collectives, local(): modulation = lax.all_gather(mod_local, 'tensor', axis=2, tiled=True)  90.7 us
    unnamed x176, local copies, waits for them, and re-layouts  57.3 us
  transfers between devices with their start and end apart: 5, of which 5 were waited for; matrix products, arithmetic and copies ran while one was open for 4% of the time, Pallas kernels for 0%

profile of v1, /device:TPU:0, one launch (start us, length us, event | category | flops | bytes accessed | tf_op | source)
XLA Modules:
  0.0 2422.9 jit_solution(9778393584793108920)
XLA Ops:
  10.5 4.5 fusion.14
  19.4 90.7 %all_gather.9 = f32[8,6,1152]{1,0,2:T(8,128)} all-gather(f32[8,6,288]{1,0,2:T(8,128)} %copy.75), channel_id=1, replica_groups=mesh['dp'=8,'tensor'=4] {'tensor'}, dimensions={2}, use_global_device_ids=true | all-gather | bytes 276480 | tf_op jit(solution)/shard_map/all_gather | solution.py:77
  110.1 22.0 fusion.73
  138.9 7.8 fusion.40
  159.1 5.6 fusion.49
  179.8 310.3 %all-reduce.9.cloned.1.call-done = f32[8,256,1152]{2,1,0:T(8,128)} async-done(((f32[8,256,1152]{2,1,0:T(8,128)}), f32[8,256,1152]{2,1,0:T(8,128)}) %all-reduce.9.cloned.1.call-update) | async-done | bytes 9437200 | tf_op jit(solution)/shard_map/psum | solution.py:104
  490.1 10.4 fusion.71
  500.5 4.9 multiply_reduce_fusion.4
  506.8 9.6 fusion.35
  516.5 12.8 convert_reduce_fusion.2
  531.4 9.4 fusion.33
  541.6 13.9 fusion.31
  555.5 615.9 %all-gather.3.cloned.1.call-done = f32[32,256,1152]{2,1,0:T(8,128)} async-done(((f32[8,256,1152]{2,1,0:T(8,128)}), f32[32,256,1152]{2,1,0:T(8,128)}) %all-gather.3.cloned.1.call-update) | async-done | bytes 37748752 | tf_op jit(solution)/shard_map/all_gather | solution.py:57
  1171.4 17.6 reduce_sum.212
  1188.9 8.3 multiply_reduce_fusion.1
  1198.1 11.5 convert_reduce_fusion.3
  1225.2 8.0 convolution_bitcast_fusion.2
  1233.8 16.6 convolution_bitcast_fusion
  1250.4 13.4 reduce.1
  1263.9 597.4 %all-reduce.15.cloned.1.call-done = (f32[8,256,1152]{2,1,0:T(8,128)}, f32[8,256,1152]{2,1,0:T(8,128)}) async-done(((f32[8,256,1152]{2,1,0:T(8,128)}, f32[8,256,1152]{2,1,0:T(8,128)}), (f32[8,256,1152]{2,1,0:T(8,128)}, f32[8,256,1152]{2,1,0:T(8,128)})) %all-reduce.15.cloned.1.call-update) | async-done | bytes 18874384 | tf_op jit(solution)/shard_map/psum | solution.py:114
  1861.4 8.6 fusion.13
  1870.0 13.2 convert_reduce_fusion.1
  1883.4 9.1 multiply_reduce_fusion.2
  1893.3 4.4 fusion.54
  1902.3 15.0 convolution_bitcast_fusion.1
  1917.4 5.3 convolution_bitcast_fusion.4
  1922.7 9.9 convolution_bitcast_fusion.3
  1932.6 4.7 fusion.56
  1938.3 24.2 %all-reduce.1 = (f32[6,288]{1,0:T(8,128)}, f32[2,288]{1,0:T(2,128)}, f32[1152]{0:T(1024)}, f32[1152]{0:T(1024)}, f32[1152]{0:T(1024)}) all-reduce(f32[6,288]{1,0:T(8,128)S(1)} %convert_reduce_fusion.6, f32[2,288]{1,0:T(2,128)S(1)} %pad_maximum_fusion.3, f32[1152]{0:T(1024)S(1)} %copy-done.42, ...), channel_id=1, replica_groups=mesh['dp'=8,'tensor'=4] {'dp'}, use_global_device_ids=true, to_apply=%region_25.26 | all-reduce | flops 5760 | bytes 46080 | tf_op jit(solution)/shard_map/psum | solution.py:192
  1962.5 128.3 %all-reduce.11.cloned.1.call-done = (f32[1000,1152]{1,0:T(8,128)}, f32[1001,1152]{1,0:T(8,128)}) async-done(((f32[1000,1152]{1,0:T(8,128)}, f32[1001,1152]{1,0:T(8,128)}), (f32[1000,1152]{1,0:T(8,128)}, f32[1001,1152]{1,0:T(8,128)})) %all-reduce.11.cloned.1.call-update) | async-done | bytes 9220624 | tf_op jit(solution)/shard_map/psum | solution.py:209
  2090.9 300.5 %all-reduce.13.cloned.1.call-done = (f32[1152,6,288]{0,2,1:T(8,128)}, f32[1152,3,288]{0,2,1:T(8,128)}, f32[288,1152]{1,0:T(8,128)}, f32[1152,1152]{1,0:T(8,128)}, f32[1152,1152]{1,0:T(8,128)}) async-done(((f32[1152,6,288]{0,2,1:T(8,128)}, f32[1152,3,288]{0,2,1:T(8,128)}, f32[288,1152]{1,0:T(8,128)}, f32[1152,1152]{1,0:T(8,128)}, f32[1152,1152]{1,0:T(8,128)}), (f32[1152,6,288]{0,2,1:T(8,128)}, ...) | async-done | bytes 23887888 | tf_op jit(solution)/shard_map/psum | solution.py:192
  2391.3 5.1 copy.123
  (236 shorter events, 88.1 us)
Async XLA Ops:
  7.2 509.3 %copy-start = (bf16[1152,1152]{1,0:T(8,128)(2,1)S(1)}, bf16[1152,1152]{1,0:T(8,128)(2,1)}, u32[]{:S(2)}) copy-start(bf16[1152,1152]{1,0:T(8,128)(2,1)} %param.32) | copy-start | bytes 7962628
  7.2 482.9 %all-reduce.9.cloned.1.call-start = ((), (), s32[]{:S(2)}) async-start(), calls=%async_computation | async-start | bytes 18874368 | tf_op jit(solution)/shard_map/psum | solution.py:104
  7.3 9.3 copy-start.6
  10.5 128.3 %copy-start.32 = (f32[8,256]{1,0:T(8,128)}, f32[8,256]{1,0:T(8,128)S(1)}, u32[]{:S(2)}) copy-start(f32[8,256]{1,0:T(8,128)S(1)} %broadcast_multiply_fusion.5) | copy-start | bytes 24580
  15.0 123.8 %copy-start.34 = (f32[8,256]{1,0:T(8,128)}, f32[8,256]{1,0:T(8,128)S(1)}, u32[]{:S(2)}) copy-start(f32[8,256]{1,0:T(8,128)S(1)} %add_rsqrt_fusion.1) | copy-start | bytes 24580
  135.5 11.2 copy-start.38
  164.8 1006.6 %all-gather.3.cloned.1.call-start = ((), (), s32[]{:S(2)}) async-start(), calls=%async_computation.1 | async-start | bytes 47185920 | tf_op jit(solution)/shard_map/all_gather | solution.py:57
  165.5 324.6 %copy-start.36 = (f32[1152]{0:T(1024)}, f32[1152]{0:T(1024)S(1)}, u32[]{:S(2)}) copy-start(f32[1152]{0:T(1024)S(1)} %convert_element_type.142) | copy-start | bytes 13828
  179.7 336.7 %copy-start.55 = (f32[8]{0:T(128)}, f32[8]{0:T(128)S(1)}, u32[]{:S(2)}) copy-start(f32[8]{0:T(128)S(1)} %compare_convert_fusion) | copy-start | bytes 100
  490.1 15.3 copy-start.58
  500.5 16.0 slice-start.10
  506.8 9.6 slice-start.11
  540.8 1320.5 %all-reduce.15.cloned.1.call-start = ((), (), s32[]{:S(2)}) async-start(), calls=%async_computation.4 | async-start | bytes 37748736 | tf_op jit(solution)/shard_map/psum | solution.py:114
  1233.1 857.7 %all-reduce.11.cloned.1.call-start = ((), (), s32[]{:S(2)}) async-start(), calls=%async_computation.2 | async-start | bytes 18505728 | tf_op jit(solution)/shard_map/psum | solution.py:209
  1250.4 610.9 %copy-start.29 = (f32[8,1152]{1,0:T(8,128)S(1)}, f32[8,1152]{1,0:T(8,128)}, u32[]{:S(2)}) copy-start(f32[8,1152]{1,0:T(8,128)} %copy-done.28) | copy-start | bytes 110596
  1250.4 610.9 %copy-start.33 = (f32[8,256]{1,0:T(8,128)S(1)}, f32[8,256]{1,0:T(8,128)}, u32[]{:S(2)}) copy-start(f32[8,256]{1,0:T(8,128)} %copy-done.32) | copy-start | bytes 24580
  1250.4 610.9 %copy-start.35 = (f32[8,256]{1,0:T(8,128)S(1)}, f32[8,256]{1,0:T(8,128)}, u32[]{:S(2)}) copy-start(f32[8,256]{1,0:T(8,128)} %copy-done.34) | copy-start | bytes 24580
  1861.3 22.0 slice-start.2
  1861.3 22.0 slice-start.4
  1861.3 22.0 slice-start.5
  1861.3 22.0 slice-start.7
  1861.3 22.0 slice-start.8
  1870.0 13.3 slice-start.3
  1870.0 13.3 slice-start.6
  1870.0 13.3 slice-start.9
  1870.0 13.3 copy-start.37
  1883.4 9.2 copy-start.7
  1883.4 9.2 copy-start.27
  1883.4 9.9 copy-start.52
  1902.1 15.3 copy-start.18
  1902.1 489.3 %all-reduce.13.cloned.1.call-start = ((), (), s32[]{:S(2)}) async-start(), calls=%async_computation.3 | async-start | bytes 47775744 | tf_op jit(solution)/shard_map/psum | solution.py:192
  2396.5 12.5 slice-start.16
  (52 other events, 252.6 us)
Sparse Core Ops, SparseCore 0:
  164.9 325.1 all-reduce.8
  540.9 630.3 all-gather.2
  1233.3 627.9 all-reduce.14
  1902.2 188.6 all-reduce.10
  2096.6 294.6 all-reduce.12
